TPU v7x, 32 devices: a whole 2x2x4 slice. The times are simulated.
32 devices in a mesh: parts: 2 (over x), view: 8 (over z, y), slab: 2 (over core).
Axes of the slice: x: 2, y: 2, z: 4, core: 2. Of those that a mesh axis runs over, the one named last changes fastest.
Arguments:
- activity: bfloat16 [128, 32, 256], P(('parts', 'view'), 'slab'), parts along dimension 0, may hold values from 0.6 to 11.2
- histo_counts: int32 [32, 64, 32, 256], P(('parts', 'view'), None, 'slab'), parts along dimension 0, may hold values from 0 to 22
- background: bfloat16 [32, 32, 256], P(('parts', 'view'), 'slab'), parts along dimension 0, may hold values from 0.5 to 2
- blur_values: bfloat16 [16, 3, 256, 32], P('view'), may hold values from 0.0041503906 to 0.020751953
- band_start: int32 [16, 3, 256], P('view'), may hold values from 0 to 224, as said below
Outputs:
- gradient: float32 [128, 32, 256], P(('parts', 'view'), 'slab'), parts along dimension 0
There are 2 independent parts, one for each index of `parts`. A program takes and returns all parts, laid end to end along the dimension named above; an argument that names none is the same for every part. Nothing has to cross between parts.
Inputs may be any that keep to these rules, and one draw needn't show every extreme that they name: Each band lies inside the matrix: columns band_start to band_start + 31.
All inputs are finite; a program needn't handle non-finite values.
Results may differ from a plain program's by a relative error of at most 0.0003.
Values may be sent and summed in bfloat16 or wider, within the bound.
A program may use at most 64 MiB of HBM per device.

v0:
```python
import jax
import jax.numpy as jnp
from jax import lax
from jax.sharding import PartitionSpec as P


def padded_2(shard, sides, width):
    for axis, dim in sides:
        size, length = (lax.axis_size(axis), shard.shape[dim])
        up = [(i, (i + 1) % size) for i in range(size - 1)]
        down = [(j, i) for i, j in up]
        last = lax.slice_in_dim(shard, length - width, length, axis=dim)
        leading = lax.slice_in_dim(shard, 0, width, axis=dim)
        before = lax.ppermute(last, axis, up)
        after = lax.ppermute(leading, axis, down)
        shard = jnp.concatenate([before, shard, after], axis=dim)
    return shard


def blur_matrix(band_values, band_starts):
    width_x = band_values.shape[0]
    band_width = band_values.shape[1]
    columns = jnp.arange(width_x, dtype=jnp.int32)
    distance = columns[None, :] - band_starts[:, None]
    selector = (
        distance[:, :, None] == jnp.arange(band_width, dtype=jnp.int32)[None, None, :]
    ).astype(jnp.float32)
    return jnp.einsum("ik,ijk->ij", band_values.astype(jnp.float32), selector).astype(jnp.bfloat16)


def per_device(activity, histo_counts, background, blur_values, band_start):
    source = padded_2(activity, (("slab", 1),), 1)
    gathered = lax.all_gather(source, "view", axis=0, tiled=True)
    rows_y = gathered.shape[0]
    slices = gathered.shape[1] - 2
    width_x = gathered.shape[2]
    prepared = []
    for view_index in range(histo_counts.shape[0]):
        matrices = [
            blur_matrix(blur_values[view_index, tap_index], band_start[view_index, tap_index])
            for tap_index in range(3)
        ]
        summed = jnp.zeros((rows_y * slices, width_x), jnp.float32)
        for tap_index in range(3):
            shifted = gathered[:, tap_index : tap_index + slices, :].reshape(-1, width_x)
            summed = summed + jnp.dot(
                shifted, matrices[tap_index].T, preferred_element_type=jnp.float32
            )
        expected = (
            summed.reshape(rows_y, slices, width_x)
            + background[view_index].astype(jnp.float32)[None]
        )
        ratio_bf = (histo_counts[view_index].astype(jnp.float32) / expected - 1.0).astype(
            jnp.bfloat16
        )
        widened = padded_2(ratio_bf, (("slab", 1),), 1)
        edge_terms = None
        prepared.append((widened, matrices, edge_terms))
    gathered_sum = jnp.zeros((rows_y, slices, width_x), jnp.float32)
    for widened, matrices, edge_terms in prepared:
        back_sum = jnp.zeros((rows_y * slices, width_x), jnp.float32)
        for tap_index in range(3):
            shifted = widened[:, 2 - tap_index : 2 - tap_index + slices, :].reshape(-1, width_x)
            back_sum = back_sum + jnp.dot(
                shifted, matrices[tap_index], preferred_element_type=jnp.float32
            )
        back_sum = back_sum.reshape(rows_y, slices, width_x)
        gathered_sum = gathered_sum + back_sum
    return lax.psum_scatter(gathered_sum, "view", scatter_dimension=0, tiled=True)


def solution(mesh):
    placed = (
        P(("parts", "view"), "slab", None),
        P(("parts", "view"), None, "slab", None),
        P(("parts", "view"), "slab", None),
        P("view", None, None, None),
        P("view", None, None),
    )
    return jax.shard_map(
        per_device,
        mesh=mesh,
        in_specs=placed,
        out_specs=P(("parts", "view"), "slab", None),
        check_vma=False,
    )
```

profile of v0, /device:TPU:0, one launch (start us, length us, event | category | flops | bytes accessed | tf_op | source)
XLA Modules:
  0.0 152.9 jit_solution(17783178895907580288)
XLA Ops:
  6.5 0.0 reduce-scatter.2.cloned.1.call-start
  6.5 0.9 copy.45
  7.4 1.3 collective-permute-start.1
  8.7 0.0 copy-start.6
  8.7 0.0 copy-start.8
  8.7 3.2 %collective-permute-start = (bf16[8,1,256]{2,0,1:T(8,128)(2,1)S(1)}, bf16[8,1,256]{2,0,1:T(8,128)(2,1)S(1)}, u32[]{:S(2)}, u32[]{:S(2)}) collective-permute-start(bf16[8,1,256]{2,0,1:T(8,128)(2,1)S(1)} %get-tuple-element.26), channel_id=1, source_target_pairs={{0,1},{2,3},{4,5},{6,7},{8,9},{10,11},{12,13},{14,15},{16,17},{18,... | collective-permute-start | bytes 12296 | tf_op jit(solution)/shard_map/ppermute | solution.py:14
  11.9 1.8 %slice_convert_fusion.1 = (f32[1,64,16,256]{3,2,1,0:T(8,128)S(1)}, f32[1,64,16,256]{3,2,1,0:T(8,128)S(1)}) fusion(s32[2,64,16,256]{3,2,1,0:T(8,128)} %param.6), kind=kLoop, calls=%fused_computation.42 | loop fusion | flops 524288 | bytes 4194304 | tf_op jit(solution)/shard_map/convert_element_type | solution.py:53
  13.7 0.0 copy-done.6
  13.7 0.8 copy.51
  14.5 0.0 copy-done.8
  14.5 0.1 iota_subtract_fusion.5
  14.6 0.8 copy.53
  15.4 0.1 iota_subtract_fusion.4
  15.5 0.8 copy.55
  16.3 0.1 iota_subtract_fusion.3
  16.4 0.8 copy.57
  17.2 0.1 iota_subtract_fusion.2
  17.3 0.8 copy.59
  18.0 0.1 iota_subtract_fusion.1
  18.1 0.8 copy.61
  18.9 0.1 iota_subtract_fusion
  19.0 2.4 %fusion = bf16[256,1,256]{2,1,0:T(2,128)(2,1)S(1)} fusion(bf16[256,32,1]{1,2,0:T(2,128)(2,1)} %copy.51, s32[256,256]{1,0:T(8,128)S(1)} %iota_subtract_fusion.5), kind=kOutput, calls=%fused_computation.6 | convolution fusion | flops 6291456 | bytes 409600 | tf_op jit(solution)/shard_map/ik,ijk->ij/dot_general | solution.py:28
  21.4 1.4 fusion.1
  22.9 1.4 fusion.2
  24.3 1.4 fusion.3
  25.8 0.0 copy-done.4
  25.8 1.4 fusion.4
  27.2 1.4 fusion.5
  28.7 0.0 collective-permute-done.1
  28.7 0.0 collective-permute-done
  28.7 33.7 %all_gather.3 = bf16[64,18,256]{2,0,1:T(8,128)(2,1)S(1)} all-gather(bf16[8,18,256]{2,0,1:T(8,128)(2,1)S(1)} %pad_maximum_fusion.4), channel_id=1, replica_groups=mesh['parts'=2,'view'=8,'slab'=2] {'view'}, dimensions={0}, use_global_device_ids=true | all-gather | bytes 663552 | tf_op jit(solution)/shard_map/all_gather | solution.py:33
  62.4 0.2 fusion.31
  62.6 0.3 copy.63
  62.9 0.3 copy.64
  63.2 0.3 copy.65
  63.5 0.3 fusion.25
  63.8 0.3 fusion.28
  64.2 0.3 convolution_add_fusion.5
  64.5 0.3 convolution_add_fusion.2
  64.8 0.4 fusion.22
  65.3 0.0 copy-start
  65.3 0.4 fusion.17
  65.7 1.2 copy-done
  66.9 0.6 fusion.24
  67.4 0.1 fusion.33
  67.6 1.3 collective-permute-start.4
  68.9 3.0 %collective-permute-start.5 = (bf16[64,1,256]{2,1,0:T(2,128)(2,1)S(1)}, bf16[64,1,256]{2,1,0:T(2,128)(2,1)S(1)}, u32[]{:S(2)}, u32[]{:S(2)}) collective-permute-start(bf16[64,1,256]{2,1,0:T(2,128)(2,1)S(1)} %get-tuple-element.19), channel_id=1, source_target_pairs={{0,1},{2,3},{4,5},{6,7},{8,9},{10,11},{12,13},{14,15},{16,17},{18,... | collective-permute-start | bytes 98312 | tf_op jit(solution)/shard_map/ppermute | solution.py:14
  71.9 0.3 fusion.29
  72.2 0.1 fusion.32
  72.3 1.3 collective-permute-start.2
  73.6 3.0 %collective-permute-start.3 = (bf16[64,1,256]{2,1,0:T(2,128)(2,1)S(1)}, bf16[64,1,256]{2,1,0:T(2,128)(2,1)S(1)}, u32[]{:S(2)}, u32[]{:S(2)}) collective-permute-start(bf16[64,1,256]{2,1,0:T(2,128)(2,1)S(1)} %get-tuple-element.15), channel_id=1, source_target_pairs={{0,1},{2,3},{4,5},{6,7},{8,9},{10,11},{12,13},{14,15},{16,17},{18,... | collective-permute-start | bytes 98312 | tf_op jit(solution)/shard_map/ppermute | solution.py:14
  76.7 0.3 fusion.26
  77.0 0.0 collective-permute-done.4
  77.0 0.0 collective-permute-done.5
  77.0 0.5 pad_maximum_fusion.1
  77.5 0.3 fusion.30
  77.8 0.0 collective-permute-done.2
  77.8 0.0 collective-permute-done.3
  77.8 0.5 pad_maximum_fusion.3
  78.3 0.3 fusion.27
  78.7 0.3 fusion.12
  79.0 1.3 fusion.14
  80.3 0.0 reduce-scatter.2.cloned.1.call-update
  80.3 65.7 %reduce-scatter.2.cloned.1.call-done = f32[8,16,256]{2,1,0:T(8,128)} async-done(((f32[64,16,256]{2,1,0:T(8,128)}), f32[8,16,256]{2,1,0:T(8,128)}) %reduce-scatter.2.cloned.1.call-update) | async-done | bytes 131088 | tf_op jit(solution)/shard_map/reduce_scatter | solution.py:69
  (16 shorter events, 0.1 us)
Async XLA Ops:
  6.5 139.5 %reduce-scatter.2.cloned.1.call-start = ((), (), s32[]{:S(2)}) async-start(), calls=%async_computation.1 | async-start | bytes 1179648 | tf_op jit(solution)/shard_map/reduce_scatter | solution.py:69
  7.4 21.3 %collective-permute-start.1 = (bf16[8,1,256]{2,0,1:T(8,128)(2,1)S(1)}, bf16[8,1,256]{2,0,1:T(8,128)(2,1)S(1)}, u32[]{:S(2)}, u32[]{:S(2)}) collective-permute-start(bf16[8,1,256]{2,0,1:T(8,128)(2,1)S(1)} %get-tuple-element.27), channel_id=1, source_target_pairs={{1,0},{3,2},{5,4},{7,6},{9,8},{11,10},{13,12},{15,14},{17,16},{19,... | collective-permute-start | bytes 12296 | tf_op jit(solution)/shard_map/ppermute | solution.py:15
  8.7 5.0 %copy-start.6 = (bf16[2,3,256,32]{2,3,1,0:T(8,128)(2,1)S(1)}, bf16[2,3,256,32]{2,3,1,0:T(8,128)(2,1)}, u32[]{:S(2)}) copy-start(bf16[2,3,256,32]{2,3,1,0:T(8,128)(2,1)} %param.8) | copy-start | bytes 294916
  8.7 5.8 %copy-start.8 = (s32[2,3,256]{2,0,1:T(2,128)S(1)}, s32[2,3,256]{2,0,1:T(2,128)}, u32[]{:S(2)}) copy-start(s32[2,3,256]{2,0,1:T(2,128)} %param.9) | copy-start | bytes 18436
  8.7 20.0 %collective-permute-start = (bf16[8,1,256]{2,0,1:T(8,128)(2,1)S(1)}, bf16[8,1,256]{2,0,1:T(8,128)(2,1)S(1)}, u32[]{:S(2)}, u32[]{:S(2)}) collective-permute-start(bf16[8,1,256]{2,0,1:T(8,128)(2,1)S(1)} %get-tuple-element.26), channel_id=1, source_target_pairs={{0,1},{2,3},{4,5},{6,7},{8,9},{10,11},{12,13},{14,15},{16,17},{18,... | collective-permute-start | bytes 12296 | tf_op jit(solution)/shard_map/ppermute | solution.py:14
  19.0 2.4 %copy-start.1 = (bf16[256,32,1]{1,2,0:T(2,128)(2,1)S(1)}, bf16[256,32,1]{1,2,0:T(2,128)(2,1)}, u32[]{:S(2)}) copy-start(bf16[256,32,1]{1,2,0:T(2,128)(2,1)} %copy.53) | copy-start | bytes 49156
  21.4 1.4 copy-start.2
  22.9 1.4 copy-start.3
  24.3 1.4 copy-start.4
  25.8 1.4 copy-start.5
  27.2 1.5 copy-start.7
  65.3 1.6 %copy-start = (s32[2,64,16,256]{3,2,1,0:T(8,128)S(1)}, s32[2,64,16,256]{3,2,1,0:T(8,128)}, u32[]{:S(2)}) copy-start(s32[2,64,16,256]{3,2,1,0:T(8,128)} %param.6) | copy-start | bytes 6291460
  67.6 9.4 %collective-permute-start.4 = (bf16[64,1,256]{2,1,0:T(2,128)(2,1)S(1)}, bf16[64,1,256]{2,1,0:T(2,128)(2,1)S(1)}, u32[]{:S(2)}, u32[]{:S(2)}) collective-permute-start(bf16[64,1,256]{2,1,0:T(2,128)(2,1)S(1)} %get-tuple-element.18), channel_id=1, source_target_pairs={{1,0},{3,2},{5,4},{7,6},{9,8},{11,10},{13,12},{15,14},{17,16},{19,... | collective-permute-start | bytes 98312 | tf_op jit(solution)/shard_map/ppermute | solution.py:15
  68.9 8.1 %collective-permute-start.5 = (bf16[64,1,256]{2,1,0:T(2,128)(2,1)S(1)}, bf16[64,1,256]{2,1,0:T(2,128)(2,1)S(1)}, u32[]{:S(2)}, u32[]{:S(2)}) collective-permute-start(bf16[64,1,256]{2,1,0:T(2,128)(2,1)S(1)} %get-tuple-element.19), channel_id=1, source_target_pairs={{0,1},{2,3},{4,5},{6,7},{8,9},{10,11},{12,13},{14,15},{16,17},{18,... | collective-permute-start | bytes 98312 | tf_op jit(solution)/shard_map/ppermute | solution.py:14
  72.3 5.5 %collective-permute-start.2 = (bf16[64,1,256]{2,1,0:T(2,128)(2,1)S(1)}, bf16[64,1,256]{2,1,0:T(2,128)(2,1)S(1)}, u32[]{:S(2)}, u32[]{:S(2)}) collective-permute-start(bf16[64,1,256]{2,1,0:T(2,128)(2,1)S(1)} %get-tuple-element.14), channel_id=1, source_target_pairs={{1,0},{3,2},{5,4},{7,6},{9,8},{11,10},{13,12},{15,14},{17,16},{19,... | collective-permute-start | bytes 98312 | tf_op jit(solution)/shard_map/ppermute | solution.py:15
  73.6 4.2 %collective-permute-start.3 = (bf16[64,1,256]{2,1,0:T(2,128)(2,1)S(1)}, bf16[64,1,256]{2,1,0:T(2,128)(2,1)S(1)}, u32[]{:S(2)}, u32[]{:S(2)}) collective-permute-start(bf16[64,1,256]{2,1,0:T(2,128)(2,1)S(1)} %get-tuple-element.15), channel_id=1, source_target_pairs={{0,1},{2,3},{4,5},{6,7},{8,9},{10,11},{12,13},{14,15},{16,17},{18,... | collective-permute-start | bytes 98312 | tf_op jit(solution)/shard_map/ppermute | solution.py:14
Sparse Core Ops, SparseCore 0:
  80.5 65.5 reduce-scatter.1
where the time goes:
time: 153 us
  waiting for transfers between devices  65.7 us (43%)
  blocking collectives  33.7 us (22%)
  matrix products  14.6 us (10%)
  between operations  13.7 us (9%)
  starting transfers between devices  13.1 us (9%)
  local copies, waits for them, and re-layouts  8.04 us (5%)
  other arithmetic  4 us (3%)
    reduce_scatter x1, waiting for transfers between devices, per_device(): lax.psum_scatter(gathered_sum, 'view', scatter_dimension=0, tiled=True)  65.7 us
    all_gather x1, blocking collectives, per_device(): gathered = lax.all_gather(source, 'view', axis=0, tiled=True)  33.7 us
    dot_general x6, matrix products, blur_matrix(): jnp.einsum('ik,ijk->ij', band_values.astype(jnp.float32), selector)  9.59 us
    ppermute x3, starting transfers between devices, padded_2(): before = lax.ppermute(last, axis, up)  9.22 us
    squeeze x7, local copies, waits for them, and re-layouts, per_device(): blur_values[view_index, tap_index]  4.68 us
    ppermute x3, starting transfers between devices, padded_2(): after = lax.ppermute(leading, axis, down)  3.88 us
  transfers between devices with their start and end apart: 7, of which 1 were waited for; matrix products, arithmetic and copies ran while one was open for 12% of the time, Pallas kernels for 0%

commit v1 on v0

v1 whole, which is shorter than its diff:
```python
import functools

import jax
import jax.numpy as jnp
from jax import lax
from jax.experimental import pallas as pl
from jax.experimental.pallas import tpu as pltpu
from jax.sharding import PartitionSpec as P

MESH = pl.DeviceIdType.MESH
PAIR = 2
SLABS = 2


def kernel(
    groups, act_ref, counts_ref, back_ref, values_ref, starts_ref, out_ref,
    acts, edges, edge_own, counts, forward_w, backward_w, partial, pair_in, sums, owner_in, halo_out, halo_in,
    counts_sem, line_send, line_recv, pair_send, pair_recv, edge_send, edge_recv,
    halo_send, halo_recv, part_send, part_recv, sum_send, sum_recv,
):
    part = lax.axis_index("parts")
    view = lax.axis_index("view")
    slab = lax.axis_index("slab")
    members = groups * PAIR
    hi = view // PAIR
    lo = view % PAIR
    other = 1 - lo
    rows, slices, width = act_ref.shape
    views = back_ref.shape[0]
    taps = values_ref.shape[0] // views
    band = values_ref.shape[2]
    group_rows = PAIR * rows

    def at(hi_index, lo_index, slab_index):
        return (part, hi_index * PAIR + lo_index, slab_index)

    def ahead(step):
        return lax.rem(hi + step, groups)

    def behind(step):
        return lax.rem(hi + groups - step, groups)

    barrier = pltpu.get_barrier_semaphore()
    for step in range(members):
        pl.semaphore_signal(
            barrier, inc=1, device_id=(part, lax.rem(view + step, members), 1 - slab), device_id_type=MESH
        )
    for step in range(1, groups):
        pl.semaphore_signal(barrier, inc=1, device_id=at(ahead(step), lo, slab), device_id_type=MESH)
    pl.semaphore_signal(barrier, inc=1, device_id=at(hi, other, slab), device_id_type=MESH)

    def counts_copy(step):
        first = pl.multiple_of(behind(step) * group_rows, group_rows)
        return pltpu.make_async_copy(
            counts_ref.at[:, pl.ds(first, group_rows)], counts.at[step], counts_sem.at[step]
        )

    for step in range(groups):
        counts_copy(step).start()

    own = act_ref[...]
    own_wide = own.astype(jnp.float32)
    edge_own[...] = jnp.where(slab == 0, own_wide[:, slices - 1, :], own_wide[:, 0, :]).astype(jnp.bfloat16)
    acts[view] = own

    lane = lax.broadcasted_iota(jnp.int32, (width, 128), 1)

    def build(which):
        line = jnp.broadcast_to(starts_ref[which : which + 1, :].astype(jnp.float32), (128, width))
        start = line.T.astype(jnp.int32)
        turned = jnp.concatenate(
            [values_ref[which].astype(jnp.float32), jnp.zeros((width, 128 - band), jnp.float32)], axis=1
        )
        shift = 1
        while shift < 128:
            turned = jnp.where((start & shift) != 0, pltpu.roll(turned, shift, axis=1), turned)
            shift *= 2
        pieces = []
        for first in range(0, width, 128):
            distance = lane + first - start
            pieces.append(jnp.where((distance >= 0) & (distance < band), turned, 0.0))
        matrix = jnp.concatenate(pieces, axis=1)
        view_index, tap = which // taps, which % taps
        backward_w[view_index * width : (view_index + 1) * width, tap * width : (tap + 1) * width] = (
            matrix.astype(jnp.bfloat16)
        )
        forward_w[tap * width : (tap + 1) * width, view_index * width : (view_index + 1) * width] = (
            matrix.T.astype(jnp.bfloat16)
        )

    total = views * taps
    for which in range(total // 2):
        build(which)

    pl.semaphore_wait(barrier, members + groups)

    def pair_copy(step, source):
        return pltpu.make_async_remote_copy(
            src_ref=source, dst_ref=acts.at[behind(step) * PAIR + lo],
            send_sem=pair_send.at[step], recv_sem=pair_recv.at[step],
            device_id=at(hi, other, slab), device_id_type=MESH,
        )

    def line_copy(step):
        return pltpu.make_async_remote_copy(
            src_ref=act_ref, dst_ref=acts.at[view],
            send_sem=line_send.at[step], recv_sem=line_recv.at[step],
            device_id=at(ahead(step), lo, slab), device_id_type=MESH,
        )

    def edge_copy(step):
        return pltpu.make_async_remote_copy(
            src_ref=edge_own, dst_ref=edges.at[view],
            send_sem=edge_send.at[step], recv_sem=edge_recv.at[step],
            device_id=(part, lax.rem(view + step, members), 1 - slab), device_id_type=MESH,
        )

    pair_copy(0, act_ref).start()
    for step in range(1, groups):
        line_copy(step).start()
    for step in range(members):
        edge_copy(step).start()

    for which in range(total // 2, total):
        build(which)

    for step in range(members):
        edge_copy(step).wait_recv()

    slice_at = lax.broadcasted_iota(jnp.int32, (group_rows, slices, width), 1)
    inner = jnp.where(slab == 0, slices - 1, 0)

    def halo_copy(step):
        return pltpu.make_async_remote_copy(
            src_ref=halo_out.at[step], dst_ref=halo_in.at[step],
            send_sem=halo_send.at[step], recv_sem=halo_recv.at[step],
            device_id=at(hi, lo, 1 - slab), device_id_type=MESH,
        )

    def part_copy(step):
        return pltpu.make_async_remote_copy(
            src_ref=partial.at[step, other], dst_ref=pair_in.at[step],
            send_sem=part_send.at[step], recv_sem=part_recv.at[step],
            device_id=at(hi, other, slab), device_id_type=MESH,
        )

    def sum_copy(step):
        return pltpu.make_async_remote_copy(
            src_ref=sums.at[step], dst_ref=owner_in.at[step],
            send_sem=sum_send.at[step], recv_sem=sum_recv.at[step],
            device_id=at(behind(step), lo, slab), device_id_type=MESH,
        )

    def relay(step):
        line_copy(step).wait_recv()
        pair_copy(step, acts.at[behind(step) * PAIR + lo]).start()

    def reduce_pair(step):
        part_copy(step).wait_recv()
        sums[step] = partial[step, lo] + pair_in[step]

    def one_group(step, carry):
        @pl.when(step + 1 < groups)
        def _():
            relay(step + 1)

        group = behind(step)
        pair_copy(step, act_ref).wait_recv()
        image = acts[pl.ds(group * PAIR, PAIR)].astype(jnp.float32).reshape(group_rows, slices, width)
        edge = edges[pl.ds(group * PAIR, PAIR)].astype(jnp.float32).reshape(group_rows, 1, width)
        lower = jnp.where(slice_at == 0, jnp.where(slab == 0, 0.0, edge), pltpu.roll(image, 1, axis=1))
        upper = jnp.where(
            slice_at == slices - 1, jnp.where(slab == 0, edge, 0.0), pltpu.roll(image, slices - 1, axis=1)
        )
        stacked = jnp.concatenate(
            [x.reshape(-1, width).astype(jnp.bfloat16) for x in (lower, image, upper)], axis=1
        )
        summed = jnp.dot(stacked, forward_w[...], preferred_element_type=jnp.float32)
        counts_copy(step).wait()
        ratios = []
        ratio_edges = []
        for view_index in range(views):
            expected = (
                summed[:, view_index * width : (view_index + 1) * width].reshape(group_rows, slices, width)
                + back_ref[view_index].astype(jnp.float32)[None]
            )
            ratio = counts[step, view_index].astype(jnp.float32) / expected - 1.0
            ratio_edges.append(
                jnp.where(slab == 0, ratio[:, slices - 1, :], ratio[:, 0, :]).astype(jnp.bfloat16)
            )
            ratios.append(ratio.reshape(-1, width).astype(jnp.bfloat16))
        outer = pl.multiple_of((1 - slab) * ((taps - 1) * width), width)
        halo_out[step] = jnp.dot(
            jnp.concatenate(ratio_edges, axis=1), backward_w[:, pl.ds(outer, width)],
            preferred_element_type=jnp.float32,
        )
        halo_copy(step).start()
        spread = jnp.dot(
            jnp.concatenate(ratios, axis=1), backward_w[...], preferred_element_type=jnp.float32
        ).reshape(group_rows, slices, taps * width)
        from_upper = pltpu.roll(spread[:, :, :width], slices - 1, axis=1)
        from_lower = pltpu.roll(spread[:, :, 2 * width :], 1, axis=1)
        halo_copy(step).wait_recv()
        halo = halo_in[step].reshape(group_rows, 1, width)
        from_upper = jnp.where(slice_at == slices - 1, jnp.where(slab == 0, halo, 0.0), from_upper)
        from_lower = jnp.where(slice_at == 0, jnp.where(slab == 0, 0.0, halo), from_lower)
        partial[step] = (spread[:, :, width : 2 * width] + from_upper + from_lower).reshape(
            PAIR, rows, slices, width
        )
        part_copy(step).start()

        @pl.when(step > 0)
        def _():
            reduce_pair(step - 1)

        @pl.when(step > 1)
        def _():
            sum_copy(step - 1).start()

        return carry

    lax.fori_loop(0, groups, one_group, 0)
    reduce_pair(groups - 1)
    if groups > 1:
        sum_copy(groups - 1).start()
    gradient = sums[0]
    for step in range(1, groups):
        sum_copy(step).wait_recv()
        gradient = gradient + owner_in[step]
    out_ref[...] = gradient

    for step in range(1, groups):
        line_copy(step).wait_send()
        sum_copy(step).wait_send()
    for step in range(groups):
        pair_copy(step, act_ref).wait_send()
        halo_copy(step).wait_send()
        part_copy(step).wait_send()
    for step in range(members):
        edge_copy(step).wait_send()


def per_device(activity, histo_counts, background, blur_values, band_start):
    members = lax.axis_size("view")
    groups = members // PAIR
    rows, slices, width = activity.shape
    views, taps, _, band = blur_values.shape
    group_rows = PAIR * rows
    dma = pltpu.SemaphoreType.DMA
    block = (rows, slices, width)
    vmem = pl.BlockSpec(memory_space=pltpu.VMEM)
    return pl.pallas_call(
        functools.partial(kernel, groups),
        out_shape=jax.ShapeDtypeStruct(block, jnp.float32),
        in_specs=[vmem, pl.BlockSpec(memory_space=pl.ANY), vmem, vmem, vmem],
        out_specs=vmem,
        scratch_shapes=[
            pltpu.VMEM((members,) + block, jnp.bfloat16),
            pltpu.VMEM((members, rows, width), jnp.bfloat16),
            pltpu.VMEM((rows, width), jnp.bfloat16),
            pltpu.VMEM((groups, views, group_rows, slices, width), jnp.int32),
            pltpu.VMEM((taps * width, views * width), jnp.bfloat16),
            pltpu.VMEM((views * width, taps * width), jnp.bfloat16),
            pltpu.VMEM((groups, PAIR) + block, jnp.float32),
            pltpu.VMEM((groups,) + block, jnp.float32),
            pltpu.VMEM((groups,) + block, jnp.float32),
            pltpu.VMEM((groups,) + block, jnp.float32),
            pltpu.VMEM((groups, group_rows, width), jnp.float32),
            pltpu.VMEM((groups, group_rows, width), jnp.float32),
            dma((groups,)),
            dma((groups,)), dma((groups,)),
            dma((groups,)), dma((groups,)),
            dma((members,)), dma((members,)),
            dma((groups,)), dma((groups,)),
            dma((groups,)), dma((groups,)),
            dma((groups,)), dma((groups,)),
        ],
        compiler_params=pltpu.CompilerParams(collective_id=0, has_side_effects=True, vmem_limit_bytes=60 << 20),
        name="poisson_gradient",
    )(
        activity, histo_counts, background,
        blur_values.reshape(views * taps, width, band), band_start.reshape(views * taps, width),
    )


def solution(mesh):
    placed = (
        P(("parts", "view"), "slab", None),
        P(("parts", "view"), None, "slab", None),
        P(("parts", "view"), "slab", None),
        P("view", None, None, None),
        P("view", None, None),
    )
    return jax.shard_map(
        per_device,
        mesh=mesh,
        in_specs=placed,
        out_specs=P(("parts", "view"), "slab", None),
        check_vma=False,
    )
```

time: 153 us -> 47 us (0.31)
  waiting for transfers between devices: 65.7 us -> 0 us
  Pallas kernels: 0 us -> 42.1 us
  blocking collectives: 33.7 us -> 0 us
  matrix products: 14.6 us -> 0 us
  between operations: 13.7 us -> 0.01 us
  starting transfers between devices: 13.1 us -> 0 us
  other arithmetic: 4 us -> 0 us
  local copies, waits for them, and re-layouts: 8.04 us -> 4.67 us
    reduce_scatter x1 -> x0, waiting for transfers between devices: 65.7 us -> none  [per_device(): lax.psum_scatter(gathered_sum, 'view', scatter_dimension=0, tiled=True)]
    pallas_call x0 -> x1, Pallas kernels: none -> 42.1 us  [per_device(): pl.pallas_call(functools.partial(kernel, groups), out_shape=jax.ShapeDtyp...]
    all_gather x1 -> x0, blocking collectives: 33.7 us -> none  [per_device(): gathered = lax.all_gather(source, 'view', axis=0, tiled=True)]
    dot_general x18 -> x0, matrix products: 14.6 us -> none  [the longest x6 9.59 us: blur_matrix(): jnp.einsum('ik,ijk->ij', band_values.astype(jnp.float32), selector)]
    ppermute x6 -> x0, starting transfers between devices: 13.1 us -> none  [the longest x3 9.22 us: padded_2(): before = lax.ppermute(last, axis, up)]
    squeeze x7 -> x0, local copies, waits for them, and re-layouts: 4.68 us -> none  [per_device(): blur_values[view_index, tap_index]]
    convert_element_type x2 -> x0, other arithmetic: 2.38 us -> none  [the longest x1 1.79 us: per_device(): histo_counts[view_index].astype(jnp.float32) / expected - 1.0]
    unnamed x22 -> x3, local copies, waits for them, and re-layouts: 2.96 us -> 4.07 us
  transfers between devices with their start and end apart: 7 -> 0, of which waited for: 1 -> 0; matrix products, arithmetic and copies ran while one was open for 12% -> 0% of each run, Pallas kernels for 0% -> 0%
where the time goes in v1:
time: 47 us; the launch traced here: 46.8 us
  Pallas kernels  42.1 us (90%)
  local copies, waits for them, and re-layouts  4.67 us (10%)
    pallas_call x1, Pallas kernels, per_device(): pl.pallas_call(functools.partial(kernel, groups), out_shape=jax.ShapeDtyp...  42.1 us
    unnamed x3, local copies, waits for them, and re-layouts  4.07 us

profile of v1, /device:TPU:0, one launch (start us, length us, event | category | flops | bytes accessed | tf_op | source)
XLA Modules:
  0.0 46.8 jit_solution(3730773830043849190)
XLA Ops:
  0.0 0.7 %copy.9 = s32[2,3,256]{2,1,0:T(4,128)S(1)} copy(s32[2,3,256]{2,0,1:T(2,128)} %param.9) | data formatting | bytes 12288 | tf_op args[4]
  0.7 0.6 %reshape.7.starts_ref = s32[6,256]{1,0:T(8,128)} reshape(s32[2,3,256]{2,1,0:T(4,128)S(1)} %copy.9) | data formatting | bytes 12288 | tf_op jit(solution)/shard_map/reshape | solution.py:282
  1.3 1.8 %copy.8 = bf16[2,3,256,32]{3,2,1,0:T(8,128)(2,1)} copy(bf16[2,3,256,32]{2,3,1,0:T(8,128)(2,1)} %param.8) | data formatting | bytes 196608 | tf_op args[3]
  3.1 42.1 %poisson_gradient.1 = f32[8,16,256]{2,1,0:T(8,128)} custom-call(bf16[8,16,256]{2,1,0:T(8,128)(2,1)} %act_ref.1, s32[2,64,16,256]{3,2,1,0:T(8,128)} %counts_ref.1, bf16[2,16,256]{2,1,0:T(8,128)(2,1)} %back_ref.1, bf16[6,256,32]{2,1,0:T(8,128)(2,1)} %bitcast.1, s32[6,256]{1,0:T(8,128)} %reshape.7.starts_ref), custom_call_target="tpu_custom_call" | custom-call | tf_op jit(solution)/shard_map/poisson_gradient/pallas_call | solution.py:252
  45.2 1.6 %copy.11 = f32[8,16,256]{2,1,0:T(8,128)} copy(f32[8,16,256]{2,1,0:T(8,128)} %poisson_gradient.1) | data formatting | bytes 262144

commit v2 on v1

--- a/solution.py
+++ b/solution.py
@@ -28,17 +28,17 @@
     rows, slices, width = act_ref.shape
     views = back_ref.shape[0]
     taps = values_ref.shape[0] // views
-    band = values_ref.shape[2]
     group_rows = PAIR * rows
 
     def at(hi_index, lo_index, slab_index):
         return (part, hi_index * PAIR + lo_index, slab_index)
 
-    def ahead(step):
-        return lax.rem(hi + step, groups)
-
-    def behind(step):
-        return lax.rem(hi + groups - step, groups)
+    def met(step):
+        index, unit = 0, 1
+        while unit < groups:
+            index += ((hi // unit + step // unit) % 2) * unit
+            unit *= 2
+        return index
 
     barrier = pltpu.get_barrier_semaphore()
     for step in range(members):
@@ -46,11 +46,11 @@
             barrier, inc=1, device_id=(part, lax.rem(view + step, members), 1 - slab), device_id_type=MESH
         )
     for step in range(1, groups):
-        pl.semaphore_signal(barrier, inc=1, device_id=at(ahead(step), lo, slab), device_id_type=MESH)
+        pl.semaphore_signal(barrier, inc=1, device_id=at(met(step), lo, slab), device_id_type=MESH)
     pl.semaphore_signal(barrier, inc=1, device_id=at(hi, other, slab), device_id_type=MESH)
 
     def counts_copy(step):
-        first = pl.multiple_of(behind(step) * group_rows, group_rows)
+        first = pl.multiple_of(met(step) * group_rows, group_rows)
         return pltpu.make_async_copy(
             counts_ref.at[:, pl.ds(first, group_rows)], counts.at[step], counts_sem.at[step]
         )
@@ -63,40 +63,38 @@
     edge_own[...] = jnp.where(slab == 0, own_wide[:, slices - 1, :], own_wide[:, 0, :]).astype(jnp.bfloat16)
     acts[view] = own
 
-    lane = lax.broadcasted_iota(jnp.int32, (width, 128), 1)
-
     def build(which):
-        line = jnp.broadcast_to(starts_ref[which : which + 1, :].astype(jnp.float32), (128, width))
-        start = line.T.astype(jnp.int32)
+        view_index, tap = which // taps, which % taps
+        start = starts_ref[tap, view_index : view_index + 1, :]
         turned = jnp.concatenate(
-            [values_ref[which].astype(jnp.float32), jnp.zeros((width, 128 - band), jnp.float32)], axis=1
+            [values_ref[which].astype(jnp.float32), jnp.zeros((8, width), jnp.float32)], axis=0
         )
         shift = 1
-        while shift < 128:
-            turned = jnp.where((start & shift) != 0, pltpu.roll(turned, shift, axis=1), turned)
+        while shift < 8:
+            turned = jnp.where((start & shift) != 0, pltpu.roll(turned, shift, axis=0), turned)
             shift *= 2
-        pieces = []
-        for first in range(0, width, 128):
-            distance = lane + first - start
-            pieces.append(jnp.where((distance >= 0) & (distance < band), turned, 0.0))
-        matrix = jnp.concatenate(pieces, axis=1)
-        view_index, tap = which // taps, which % taps
+        while shift < width:
+            extra = min(shift, width - turned.shape[0])
+            plain = jnp.concatenate([turned, jnp.zeros((extra, width), jnp.float32)], axis=0)
+            moved = jnp.concatenate([jnp.zeros((shift, width), jnp.float32), turned], axis=0)[: plain.shape[0]]
+            turned = jnp.where((start & shift) != 0, moved, plain)
+            shift *= 2
+        forward_w[tap * width : (tap + 1) * width, view_index * width : (view_index + 1) * width] = (
+            turned.astype(jnp.bfloat16)
+        )
         backward_w[view_index * width : (view_index + 1) * width, tap * width : (tap + 1) * width] = (
-            matrix.astype(jnp.bfloat16)
-        )
-        forward_w[tap * width : (tap + 1) * width, view_index * width : (view_index + 1) * width] = (
-            matrix.T.astype(jnp.bfloat16)
+            turned.T.astype(jnp.bfloat16)
         )
 
     total = views * taps
-    for which in range(total // 2):
+    for which in range(total):
         build(which)
 
     pl.semaphore_wait(barrier, members + groups)
 
     def pair_copy(step, source):
         return pltpu.make_async_remote_copy(
-            src_ref=source, dst_ref=acts.at[behind(step) * PAIR + lo],
+            src_ref=source, dst_ref=acts.at[met(step) * PAIR + lo],
             send_sem=pair_send.at[step], recv_sem=pair_recv.at[step],
             device_id=at(hi, other, slab), device_id_type=MESH,
         )
@@ -105,27 +103,21 @@
         return pltpu.make_async_remote_copy(
             src_ref=act_ref, dst_ref=acts.at[view],
             send_sem=line_send.at[step], recv_sem=line_recv.at[step],
-            device_id=at(ahead(step), lo, slab), device_id_type=MESH,
+            device_id=at(met(step), lo, slab), device_id_type=MESH,
         )
 
     def edge_copy(step):
         return pltpu.make_async_remote_copy(
             src_ref=edge_own, dst_ref=edges.at[view],
             send_sem=edge_send.at[step], recv_sem=edge_recv.at[step],
-            device_id=(part, lax.rem(view + step, members), 1 - slab), device_id_type=MESH,
-        )
-
-    pair_copy(0, act_ref).start()
-    for step in range(1, groups):
-        line_copy(step).start()
+            device_id=at(met(step // PAIR), (lo + step % PAIR) % PAIR, 1 - slab), device_id_type=MESH,
+        )
+
     for step in range(members):
         edge_copy(step).start()
-
-    for which in range(total // 2, total):
-        build(which)
-
-    for step in range(members):
-        edge_copy(step).wait_recv()
+    pair_copy(0, act_ref).start()
+    for step in range(1, groups):
+        line_copy(step).start()
 
     slice_at = lax.broadcasted_iota(jnp.int32, (group_rows, slices, width), 1)
     inner = jnp.where(slab == 0, slices - 1, 0)
@@ -148,12 +140,12 @@
         return pltpu.make_async_remote_copy(
             src_ref=sums.at[step], dst_ref=owner_in.at[step],
             send_sem=sum_send.at[step], recv_sem=sum_recv.at[step],
-            device_id=at(behind(step), lo, slab), device_id_type=MESH,
+            device_id=at(met(step), lo, slab), device_id_type=MESH,
         )
 
     def relay(step):
         line_copy(step).wait_recv()
-        pair_copy(step, acts.at[behind(step) * PAIR + lo]).start()
+        pair_copy(step, acts.at[met(step) * PAIR + lo]).start()
 
     def reduce_pair(step):
         part_copy(step).wait_recv()
@@ -164,7 +156,9 @@
         def _():
             relay(step + 1)
 
-        group = behind(step)
+        group = met(step)
+        for which in range(PAIR):
+            edge_copy(step * PAIR + which).wait_recv()
         pair_copy(step, act_ref).wait_recv()
         image = acts[pl.ds(group * PAIR, PAIR)].astype(jnp.float32).reshape(group_rows, slices, width)
         edge = edges[pl.ds(group * PAIR, PAIR)].astype(jnp.float32).reshape(group_rows, 1, width)
@@ -252,7 +246,7 @@
     return pl.pallas_call(
         functools.partial(kernel, groups),
         out_shape=jax.ShapeDtypeStruct(block, jnp.float32),
-        in_specs=[vmem, pl.BlockSpec(memory_space=pl.ANY), vmem, vmem, vmem],
+        in_specs=[vmem, pl.BlockSpec(memory_space=pltpu.HBM), vmem, vmem, vmem],
         out_specs=vmem,
         scratch_shapes=[
             pltpu.VMEM((members,) + block, jnp.bfloat16),
@@ -275,11 +269,11 @@
             dma((groups,)), dma((groups,)),
             dma((groups,)), dma((groups,)),
         ],
-        compiler_params=pltpu.CompilerParams(collective_id=0, has_side_effects=True, vmem_limit_bytes=60 << 20),
+        compiler_params=pltpu.CompilerParams(collective_id=0, has_side_effects=True, vmem_limit_bytes=36 << 20),
         name="poisson_gradient",
     )(
         activity, histo_counts, background,
-        blur_values.reshape(views * taps, width, band), band_start.reshape(views * taps, width),
+        jnp.swapaxes(blur_values, 2, 3).reshape(views * taps, band, width), jnp.swapaxes(band_start, 0, 1),
     )
 
 

time: 47 us -> 42 us (0.89); the launches traced: 46.8 us -> 41.3 us
  Pallas kernels: 42.1 us -> 35.9 us
  local copies, waits for them, and re-layouts: 4.67 us -> 5.39 us
    pallas_call x1, Pallas kernels: 42.1 us -> 35.9 us  [per_device(): pl.pallas_call(functools.partial(kernel, groups), out_shape=jax.ShapeDtyp...]
    unnamed x3 -> x11, local copies, waits for them, and re-layouts: 4.07 us -> 5.39 us
    reshape x1 -> x0, local copies, waits for them, and re-layouts: 0.61 us -> none  [per_device(): band_start.reshape(views * taps, width)]
where the time goes in v2:
time: 42 us; the launch traced here: 41.3 us
  Pallas kernels  35.9 us (85%)
  local copies, waits for them, and re-layouts  5.39 us (13%)
    pallas_call x1, Pallas kernels, per_device(): pl.pallas_call(functools.partial(kernel, groups), out_shape=jax.ShapeDtyp...  35.9 us
    unnamed x11, local copies, waits for them, and re-layouts  5.39 us

profile of v2, /device:TPU:0, one launch (start us, length us, event | category | flops | bytes accessed | tf_op | source)
XLA Modules:
  0.0 41.3 jit_solution(15315069931098695784)
XLA Ops:
  0.0 0.0 copy-start
  0.0 1.6 %copy-done = s32[2,64,16,256]{3,2,1,0:T(8,128)S(1)} copy-done((s32[2,64,16,256]{3,2,1,0:T(8,128)S(1)}, s32[2,64,16,256]{3,2,1,0:T(8,128)}, u32[]{:S(2)}) %copy-start) | copy-done | bytes 2097176
  1.6 0.0 copy-start.1
  1.6 0.9 %copy-done.1 = bf16[2,3,256,32]{2,3,1,0:T(8,128)(2,1)S(1)} copy-done((bf16[2,3,256,32]{2,3,1,0:T(8,128)(2,1)S(1)}, bf16[2,3,256,32]{2,3,1,0:T(8,128)(2,1)}, u32[]{:S(2)}) %copy-start.1) | copy-done | bytes 98328
  2.5 0.0 copy-start.2
  2.5 0.8 %copy-done.2 = bf16[8,16,256]{2,1,0:T(8,128)(2,1)S(1)} copy-done((bf16[8,16,256]{2,1,0:T(8,128)(2,1)S(1)}, bf16[8,16,256]{2,1,0:T(8,128)(2,1)}, u32[]{:S(2)}) %copy-start.2) | copy-done | bytes 65560
  3.3 0.0 copy-start.3
  3.3 0.7 %copy-done.3 = bf16[2,16,256]{2,1,0:T(8,128)(2,1)S(1)} copy-done((bf16[2,16,256]{2,1,0:T(8,128)(2,1)S(1)}, bf16[2,16,256]{2,1,0:T(8,128)(2,1)}, u32[]{:S(2)}) %copy-start.3) | copy-done | bytes 16408
  4.0 0.0 copy-start.4
  4.0 0.7 %copy-done.4 = s32[2,3,256]{2,0,1:T(2,128)S(1)} copy-done((s32[2,3,256]{2,0,1:T(2,128)S(1)}, s32[2,3,256]{2,0,1:T(2,128)}, u32[]{:S(2)}) %copy-start.4) | copy-done | bytes 6168
  4.7 35.9 %poisson_gradient.1 = f32[8,16,256]{2,1,0:T(8,128)S(1)} custom-call(bf16[8,16,256]{2,1,0:T(8,128)(2,1)S(1)} %copy-done.2, s32[2,64,16,256]{3,2,1,0:T(8,128)S(1)} %copy-done, bf16[2,16,256]{2,1,0:T(8,128)(2,1)S(1)} %copy-done.3, bf16[6,32,256]{2,1,0:T(8,128)(2,1)S(1)} %bitcast.4, s32[3,2,256]{2,1,0:T(2,128)S(1)} %bitcast.5), custom_call_target="tpu_custom_call" | custom-call | tf_op jit(solution)/shard_map/poisson_gradient/pallas_call | solution.py:246
  40.6 0.7 %copy.7 = f32[8,16,256]{2,1,0:T(8,128)} copy(f32[8,16,256]{2,1,0:T(8,128)S(1)} %poisson_gradient.1) | data formatting | bytes 262144
Async XLA Ops:
  0.0 1.6 %copy-start = (s32[2,64,16,256]{3,2,1,0:T(8,128)S(1)}, s32[2,64,16,256]{3,2,1,0:T(8,128)}, u32[]{:S(2)}) copy-start(s32[2,64,16,256]{3,2,1,0:T(8,128)} %counts_ref.1) | copy-start | bytes 6291460
  1.6 0.9 %copy-start.1 = (bf16[2,3,256,32]{2,3,1,0:T(8,128)(2,1)S(1)}, bf16[2,3,256,32]{2,3,1,0:T(8,128)(2,1)}, u32[]{:S(2)}) copy-start(bf16[2,3,256,32]{2,3,1,0:T(8,128)(2,1)} %param.8) | copy-start | bytes 294916
  2.5 0.8 %copy-start.2 = (bf16[8,16,256]{2,1,0:T(8,128)(2,1)S(1)}, bf16[8,16,256]{2,1,0:T(8,128)(2,1)}, u32[]{:S(2)}) copy-start(bf16[8,16,256]{2,1,0:T(8,128)(2,1)} %act_ref.1) | copy-start | bytes 196612
  3.3 0.7 %copy-start.3 = (bf16[2,16,256]{2,1,0:T(8,128)(2,1)S(1)}, bf16[2,16,256]{2,1,0:T(8,128)(2,1)}, u32[]{:S(2)}) copy-start(bf16[2,16,256]{2,1,0:T(8,128)(2,1)} %back_ref.1) | copy-start | bytes 49156
  4.0 0.7 %copy-start.4 = (s32[2,3,256]{2,0,1:T(2,128)S(1)}, s32[2,3,256]{2,0,1:T(2,128)}, u32[]{:S(2)}) copy-start(s32[2,3,256]{2,0,1:T(2,128)} %param.9) | copy-start | bytes 18436

commit v3 on v2

--- a/solution.py
+++ b/solution.py
@@ -12,11 +12,28 @@
 SLABS = 2
 
 
+CODE_MAX = 32767.0
+TINY = 1e-30
+VMEM_LIMIT = 63 << 20
+
+
+def encode(block):
+    top = jnp.max(jnp.abs(block), axis=(0, 1), keepdims=False)[None, :]
+    scale = jnp.where(top > TINY, CODE_MAX / jnp.maximum(top, TINY), 0.0)
+    code = jnp.round(block * scale[None]).astype(jnp.int32).astype(jnp.int16)
+    return code, jnp.broadcast_to(top * (1.0 / CODE_MAX), (8, block.shape[2]))
+
+
+def decode(code, unit):
+    return code.astype(jnp.int32).astype(jnp.float32) * unit[None, 0:1, :]
+
+
 def kernel(
-    groups, act_ref, counts_ref, back_ref, values_ref, starts_ref, out_ref,
-    acts, edges, edge_own, counts, forward_w, backward_w, partial, pair_in, sums, owner_in, halo_out, halo_in,
-    counts_sem, line_send, line_recv, pair_send, pair_recv, edge_send, edge_recv,
-    halo_send, halo_recv, part_send, part_recv, sum_send, sum_recv,
+    groups, act_hbm, counts_ref, back_hbm, values_hbm, starts_hbm, out_ref,
+    act_ref, back_ref, values_ref, starts_ref,
+    acts, edges, edge_own, counts, forward_w, backward_w, kept, part_code, part_unit, pair_code, pair_unit, sum_code, sum_unit, owner_code, owner_unit, halo_out, halo_in,
+    load_sem, counts_sem, line_send, line_recv, pair_send, pair_recv, edge_send, edge_recv,
+    halo_send, halo_recv, part_send, part_recv, sum_send, sum_recv, part_unit_send, part_unit_recv, sum_unit_send, sum_unit_recv,
 ):
     part = lax.axis_index("parts")
     view = lax.axis_index("view")
@@ -55,9 +72,18 @@
             counts_ref.at[:, pl.ds(first, group_rows)], counts.at[step], counts_sem.at[step]
         )
 
+    loads = [
+        pltpu.make_async_copy(source, target, load_sem.at[index])
+        for index, (source, target) in enumerate(
+            ((values_hbm, values_ref), (starts_hbm, starts_ref), (act_hbm, act_ref), (back_hbm, back_ref))
+        )
+    ]
+    for load in loads:
+        load.start()
     for step in range(groups):
         counts_copy(step).start()
-
+    for load in loads:
+        load.wait()
     own = act_ref[...]
     own_wide = own.astype(jnp.float32)
     edge_own[...] = jnp.where(slab == 0, own_wide[:, slices - 1, :], own_wide[:, 0, :]).astype(jnp.bfloat16)
@@ -129,27 +155,45 @@
             device_id=at(hi, lo, 1 - slab), device_id_type=MESH,
         )
 
-    def part_copy(step):
-        return pltpu.make_async_remote_copy(
-            src_ref=partial.at[step, other], dst_ref=pair_in.at[step],
-            send_sem=part_send.at[step], recv_sem=part_recv.at[step],
-            device_id=at(hi, other, slab), device_id_type=MESH,
-        )
-
-    def sum_copy(step):
-        return pltpu.make_async_remote_copy(
-            src_ref=sums.at[step], dst_ref=owner_in.at[step],
-            send_sem=sum_send.at[step], recv_sem=sum_recv.at[step],
-            device_id=at(met(step), lo, slab), device_id_type=MESH,
-        )
+    def part_copies(step):
+        return [
+            pltpu.make_async_remote_copy(
+                src_ref=source.at[step], dst_ref=target.at[step],
+                send_sem=send.at[step], recv_sem=recv.at[step],
+                device_id=at(hi, other, slab), device_id_type=MESH,
+            )
+            for source, target, send, recv in (
+                (part_unit, pair_unit, part_unit_send, part_unit_recv),
+                (part_code, pair_code, part_send, part_recv),
+            )
+        ]
+
+    def sum_copies(step):
+        return [
+            pltpu.make_async_remote_copy(
+                src_ref=source.at[step], dst_ref=target.at[step],
+                send_sem=send.at[step], recv_sem=recv.at[step],
+                device_id=at(met(step), lo, slab), device_id_type=MESH,
+            )
+            for source, target, send, recv in (
+                (sum_unit, owner_unit, sum_unit_send, sum_unit_recv),
+                (sum_code, owner_code, sum_send, sum_recv),
+            )
+        ]
 
     def relay(step):
         line_copy(step).wait_recv()
         pair_copy(step, acts.at[met(step) * PAIR + lo]).start()
 
-    def reduce_pair(step):
-        part_copy(step).wait_recv()
-        sums[step] = partial[step, lo] + pair_in[step]
+    def pair_sum(step):
+        for copy in part_copies(step):
+            copy.wait_recv()
+        return kept[step] + decode(pair_code[step], pair_unit[step])
+
+    def pass_on(step):
+        sum_code[step], sum_unit[step] = encode(pair_sum(step))
+        for copy in sum_copies(step):
+            copy.start()
 
     def one_group(step, carry):
         @pl.when(step + 1 < groups)
@@ -198,38 +242,39 @@
         halo = halo_in[step].reshape(group_rows, 1, width)
         from_upper = jnp.where(slice_at == slices - 1, jnp.where(slab == 0, halo, 0.0), from_upper)
         from_lower = jnp.where(slice_at == 0, jnp.where(slab == 0, 0.0, halo), from_lower)
-        partial[step] = (spread[:, :, width : 2 * width] + from_upper + from_lower).reshape(
+        spread_sum = (spread[:, :, width : 2 * width] + from_upper + from_lower).reshape(
             PAIR, rows, slices, width
         )
-        part_copy(step).start()
-
-        @pl.when(step > 0)
-        def _():
-            reduce_pair(step - 1)
+        kept[step] = jnp.where(lo == 0, spread_sum[0], spread_sum[1])
+        part_code[step], part_unit[step] = encode(jnp.where(lo == 0, spread_sum[1], spread_sum[0]))
+        for copy in part_copies(step):
+            copy.start()
 
         @pl.when(step > 1)
         def _():
-            sum_copy(step - 1).start()
+            pass_on(step - 1)
 
         return carry
 
     lax.fori_loop(0, groups, one_group, 0)
-    reduce_pair(groups - 1)
     if groups > 1:
-        sum_copy(groups - 1).start()
-    gradient = sums[0]
+        pass_on(groups - 1)
+    gradient = pair_sum(0)
     for step in range(1, groups):
-        sum_copy(step).wait_recv()
-        gradient = gradient + owner_in[step]
+        for copy in sum_copies(step):
+            copy.wait_recv()
+        gradient = gradient + decode(owner_code[step], owner_unit[step])
     out_ref[...] = gradient
 
     for step in range(1, groups):
         line_copy(step).wait_send()
-        sum_copy(step).wait_send()
+        for copy in sum_copies(step):
+            copy.wait_send()
     for step in range(groups):
         pair_copy(step, act_ref).wait_send()
         halo_copy(step).wait_send()
-        part_copy(step).wait_send()
+        for copy in part_copies(step):
+            copy.wait_send()
     for step in range(members):
         edge_copy(step).wait_send()
 
@@ -246,21 +291,31 @@
     return pl.pallas_call(
         functools.partial(kernel, groups),
         out_shape=jax.ShapeDtypeStruct(block, jnp.float32),
-        in_specs=[vmem, pl.BlockSpec(memory_space=pltpu.HBM), vmem, vmem, vmem],
+        in_specs=[pl.BlockSpec(memory_space=pl.ANY)] * 5,
         out_specs=vmem,
         scratch_shapes=[
+            pltpu.VMEM(block, jnp.bfloat16),
+            pltpu.VMEM(background.shape, jnp.bfloat16),
+            pltpu.VMEM((views * taps, band, width), jnp.bfloat16),
+            pltpu.VMEM((taps, views, width), jnp.int32),
             pltpu.VMEM((members,) + block, jnp.bfloat16),
             pltpu.VMEM((members, rows, width), jnp.bfloat16),
             pltpu.VMEM((rows, width), jnp.bfloat16),
             pltpu.VMEM((groups, views, group_rows, slices, width), jnp.int32),
             pltpu.VMEM((taps * width, views * width), jnp.bfloat16),
             pltpu.VMEM((views * width, taps * width), jnp.bfloat16),
-            pltpu.VMEM((groups, PAIR) + block, jnp.float32),
             pltpu.VMEM((groups,) + block, jnp.float32),
-            pltpu.VMEM((groups,) + block, jnp.float32),
-            pltpu.VMEM((groups,) + block, jnp.float32),
+            pltpu.VMEM((groups,) + block, jnp.int16),
+            pltpu.VMEM((groups, 8, width), jnp.float32),
+            pltpu.VMEM((groups,) + block, jnp.int16),
+            pltpu.VMEM((groups, 8, width), jnp.float32),
+            pltpu.VMEM((groups,) + block, jnp.int16),
+            pltpu.VMEM((groups, 8, width), jnp.float32),
+            pltpu.VMEM((groups,) + block, jnp.int16),
+            pltpu.VMEM((groups, 8, width), jnp.float32),
             pltpu.VMEM((groups, group_rows, width), jnp.float32),
             pltpu.VMEM((groups, group_rows, width), jnp.float32),
+            dma((4,)),
             dma((groups,)),
             dma((groups,)), dma((groups,)),
             dma((groups,)), dma((groups,)),
@@ -268,8 +323,10 @@
             dma((groups,)), dma((groups,)),
             dma((groups,)), dma((groups,)),
             dma((groups,)), dma((groups,)),
+            dma((groups,)), dma((groups,)),
+            dma((groups,)), dma((groups,)),
         ],
-        compiler_params=pltpu.CompilerParams(collective_id=0, has_side_effects=True, vmem_limit_bytes=36 << 20),
+        compiler_params=pltpu.CompilerParams(collective_id=0, has_side_effects=True, vmem_limit_bytes=VMEM_LIMIT),
         name="poisson_gradient",
     )(
         activity, histo_counts, background,

time: 42 us -> 33.4 us (0.80); the launches traced: 41.3 us -> 33.3 us
  Pallas kernels: 35.9 us -> 31.7 us
  local copies, waits for them, and re-layouts: 5.39 us -> 1.57 us
    pallas_call x1, Pallas kernels: 35.9 us -> 31.7 us  [per_device(): pl.pallas_call(functools.partial(kernel, groups), out_shape=jax.ShapeDtyp...]
    unnamed x11 -> x1, local copies, waits for them, and re-layouts: 5.39 us -> 1.57 us
where the time goes in v3:
time: 33.4 us; the launch traced here: 33.3 us
  Pallas kernels  31.7 us (95%)
  local copies, waits for them, and re-layouts  1.57 us (5%)
    pallas_call x1, Pallas kernels, per_device(): pl.pallas_call(functools.partial(kernel, groups), out_shape=jax.ShapeDtyp...  31.7 us
    unnamed x1, local copies, waits for them, and re-layouts  1.57 us

profile of v3, /device:TPU:0, one launch (start us, length us, event | category | flops | bytes accessed | tf_op | source)
XLA Modules:
  0.0 33.3 jit_solution(14127404978693461228)
XLA Ops:
  0.0 31.7 %poisson_gradient.1 = f32[8,16,256]{2,1,0:T(8,128)} custom-call(bf16[8,16,256]{2,1,0:T(8,128)(2,1)} %act_hbm.1, s32[2,64,16,256]{3,2,1,0:T(8,128)} %counts_ref.1, bf16[2,16,256]{2,1,0:T(8,128)(2,1)} %back_hbm.1, bf16[6,32,256]{2,1,0:T(8,128)(2,1)} %bitcast.4, s32[3,2,256]{2,1,0:T(2,128)} %bitcast.5), custom_call_target="tpu_custom_call" | custom-call | tf_op jit(solution)/shard_map/poisson_gradient/pallas_call | solution.py:291
  31.7 1.6 %copy.7 = f32[8,16,256]{2,1,0:T(8,128)} copy(f32[8,16,256]{2,1,0:T(8,128)} %poisson_gradient.1) | data formatting | bytes 262144

commit v4 on v3

--- a/solution.py
+++ b/solution.py
@@ -39,6 +39,7 @@
     view = lax.axis_index("view")
     slab = lax.axis_index("slab")
     members = groups * PAIR
+    last = groups - 1
     hi = view // PAIR
     lo = view % PAIR
     other = 1 - lo
@@ -51,9 +52,10 @@
         return (part, hi_index * PAIR + lo_index, slab_index)
 
     def met(step):
+        key = (groups - step) % groups
         index, unit = 0, 1
         while unit < groups:
-            index += ((hi // unit + step // unit) % 2) * unit
+            index += ((hi // unit + key // unit) % 2) * unit
             unit *= 2
         return index
 
@@ -65,6 +67,7 @@
     for step in range(1, groups):
         pl.semaphore_signal(barrier, inc=1, device_id=at(met(step), lo, slab), device_id_type=MESH)
     pl.semaphore_signal(barrier, inc=1, device_id=at(hi, other, slab), device_id_type=MESH)
+    pl.semaphore_signal(barrier, inc=1, device_id=at(met(last), other, slab), device_id_type=MESH)
 
     def counts_copy(step):
         first = pl.multiple_of(met(step) * group_rows, group_rows)
@@ -116,7 +119,7 @@
     for which in range(total):
         build(which)
 
-    pl.semaphore_wait(barrier, members + groups)
+    pl.semaphore_wait(barrier, members + groups + 1)
 
     def pair_copy(step, source):
         return pltpu.make_async_remote_copy(
@@ -125,6 +128,13 @@
             device_id=at(hi, other, slab), device_id_type=MESH,
         )
 
+    def near_copy():
+        return pltpu.make_async_remote_copy(
+            src_ref=acts.at[hi * PAIR + other], dst_ref=acts.at[hi * PAIR + other],
+            send_sem=pair_send.at[last], recv_sem=pair_recv.at[last],
+            device_id=at(met(last), lo, slab), device_id_type=MESH,
+        )
+
     def line_copy(step):
         return pltpu.make_async_remote_copy(
             src_ref=act_ref, dst_ref=acts.at[view],
@@ -148,21 +158,24 @@
     slice_at = lax.broadcasted_iota(jnp.int32, (group_rows, slices, width), 1)
     inner = jnp.where(slab == 0, slices - 1, 0)
 
-    def halo_copy(step):
-        return pltpu.make_async_remote_copy(
-            src_ref=halo_out.at[step], dst_ref=halo_in.at[step],
-            send_sem=halo_send.at[step], recv_sem=halo_recv.at[step],
-            device_id=at(hi, lo, 1 - slab), device_id_type=MESH,
-        )
-
-    def part_copies(step):
+    def halo_copies(step):
         return [
             pltpu.make_async_remote_copy(
-                src_ref=source.at[step], dst_ref=target.at[step],
+                src_ref=halo_out.at[step, keeper], dst_ref=halo_in.at[step, index],
+                send_sem=halo_send.at[step, index], recv_sem=halo_recv.at[step, index],
+                device_id=at(hi, keeper, 1 - slab), device_id_type=MESH,
+            )
+            for index, keeper in enumerate((lo, other))
+        ]
+
+    def part_copies(step, target):
+        return [
+            pltpu.make_async_remote_copy(
+                src_ref=source.at[step], dst_ref=landing.at[step],
                 send_sem=send.at[step], recv_sem=recv.at[step],
-                device_id=at(hi, other, slab), device_id_type=MESH,
-            )
-            for source, target, send, recv in (
+                device_id=at(target, other, slab), device_id_type=MESH,
+            )
+            for source, landing, send, recv in (
                 (part_unit, pair_unit, part_unit_send, part_unit_recv),
                 (part_code, pair_code, part_send, part_recv),
             )
@@ -185,25 +198,36 @@
         line_copy(step).wait_recv()
         pair_copy(step, acts.at[met(step) * PAIR + lo]).start()
 
-    def pair_sum(step):
-        for copy in part_copies(step):
+    def kept_sum(step):
+        for copy in halo_copies(step):
             copy.wait_recv()
-        return kept[step] + decode(pair_code[step], pair_unit[step])
-
-    def pass_on(step):
-        sum_code[step], sum_unit[step] = encode(pair_sum(step))
+        halo = (halo_in[step, 0] + halo_in[step, 1]).reshape(rows, 1, width)
+        return kept[step] + jnp.where(slice_at[:rows] == inner, halo, 0.0)
+
+    def pair_part(step):
+        for copy in part_copies(step, hi):
+            copy.wait_recv()
+        return decode(pair_code[step], pair_unit[step])
+
+    def pass_on(step, value):
+        sum_code[step], sum_unit[step] = encode(value)
         for copy in sum_copies(step):
             copy.start()
 
     def one_group(step, carry):
-        @pl.when(step + 1 < groups)
-        def _():
-            relay(step + 1)
-
         group = met(step)
         for which in range(PAIR):
             edge_copy(step * PAIR + which).wait_recv()
         pair_copy(step, act_ref).wait_recv()
+
+        @pl.when(step == 0)
+        def _():
+            near_copy().start()
+
+        @pl.when(step == last)
+        def _():
+            line_copy(last).wait_recv()
+
         image = acts[pl.ds(group * PAIR, PAIR)].astype(jnp.float32).reshape(group_rows, slices, width)
         edge = edges[pl.ds(group * PAIR, PAIR)].astype(jnp.float32).reshape(group_rows, 1, width)
         lower = jnp.where(slice_at == 0, jnp.where(slab == 0, 0.0, edge), pltpu.roll(image, 1, axis=1))
@@ -231,40 +255,51 @@
         halo_out[step] = jnp.dot(
             jnp.concatenate(ratio_edges, axis=1), backward_w[:, pl.ds(outer, width)],
             preferred_element_type=jnp.float32,
-        )
-        halo_copy(step).start()
+        ).reshape(PAIR, rows, width)
+        for copy in halo_copies(step):
+            copy.start()
         spread = jnp.dot(
             jnp.concatenate(ratios, axis=1), backward_w[...], preferred_element_type=jnp.float32
         ).reshape(group_rows, slices, taps * width)
         from_upper = pltpu.roll(spread[:, :, :width], slices - 1, axis=1)
         from_lower = pltpu.roll(spread[:, :, 2 * width :], 1, axis=1)
-        halo_copy(step).wait_recv()
-        halo = halo_in[step].reshape(group_rows, 1, width)
-        from_upper = jnp.where(slice_at == slices - 1, jnp.where(slab == 0, halo, 0.0), from_upper)
-        from_lower = jnp.where(slice_at == 0, jnp.where(slab == 0, 0.0, halo), from_lower)
+        from_upper = jnp.where(slice_at == slices - 1, 0.0, from_upper)
+        from_lower = jnp.where(slice_at == 0, 0.0, from_lower)
         spread_sum = (spread[:, :, width : 2 * width] + from_upper + from_lower).reshape(
             PAIR, rows, slices, width
         )
         kept[step] = jnp.where(lo == 0, spread_sum[0], spread_sum[1])
         part_code[step], part_unit[step] = encode(jnp.where(lo == 0, spread_sum[1], spread_sum[0]))
-        for copy in part_copies(step):
-            copy.start()
+
+        @pl.when(step == 0)
+        def _():
+            for later in range(1, last):
+                relay(later)
+
+        @pl.when(step < last)
+        def _():
+            for copy in part_copies(step, hi):
+                copy.start()
+
+        @pl.when(step == last)
+        def _():
+            for copy in part_copies(step, met(last)):
+                copy.start()
 
         @pl.when(step > 1)
         def _():
-            pass_on(step - 1)
+            pass_on(step - 1, kept_sum(step - 1) + pair_part(step - 1))
 
         return carry
 
     lax.fori_loop(0, groups, one_group, 0)
-    if groups > 1:
-        pass_on(groups - 1)
-    gradient = pair_sum(0)
+    pass_on(last, kept_sum(last))
+    gradient = kept_sum(0) + pair_part(0)
     for step in range(1, groups):
         for copy in sum_copies(step):
             copy.wait_recv()
         gradient = gradient + decode(owner_code[step], owner_unit[step])
-    out_ref[...] = gradient
+    out_ref[...] = gradient + pair_part(last)
 
     for step in range(1, groups):
         line_copy(step).wait_send()
@@ -272,8 +307,9 @@
             copy.wait_send()
     for step in range(groups):
         pair_copy(step, act_ref).wait_send()
-        halo_copy(step).wait_send()
-        for copy in part_copies(step):
+        for copy in halo_copies(step):
+            copy.wait_send()
+        for copy in part_copies(step, hi):
             copy.wait_send()
     for step in range(members):
         edge_copy(step).wait_send()
@@ -313,14 +349,14 @@
             pltpu.VMEM((groups, 8, width), jnp.float32),
             pltpu.VMEM((groups,) + block, jnp.int16),
             pltpu.VMEM((groups, 8, width), jnp.float32),
-            pltpu.VMEM((groups, group_rows, width), jnp.float32),
-            pltpu.VMEM((groups, group_rows, width), jnp.float32),
+            pltpu.VMEM((groups, PAIR, rows, width), jnp.float32),
+            pltpu.VMEM((groups, PAIR, rows, width), jnp.float32),
             dma((4,)),
             dma((groups,)),
             dma((groups,)), dma((groups,)),
             dma((groups,)), dma((groups,)),
             dma((members,)), dma((members,)),
-            dma((groups,)), dma((groups,)),
+            dma((groups, PAIR)), dma((groups, PAIR)),
             dma((groups,)), dma((groups,)),
             dma((groups,)), dma((groups,)),
             dma((groups,)), dma((groups,)),

time: 33.4 us -> 31.8 us (0.952)
  Pallas kernels: 31.7 us -> 30.1 us
    pallas_call x1, Pallas kernels: 31.7 us -> 30.1 us  [per_device(): pl.pallas_call(functools.partial(kernel, groups), out_shape=jax.ShapeDtyp...]
where the time goes in v4:
time: 31.8 us; the launch traced here: 31.7 us
  Pallas kernels  30.1 us (95%)
  local copies, waits for them, and re-layouts  1.57 us (5%)
    pallas_call x1, Pallas kernels, per_device(): pl.pallas_call(functools.partial(kernel, groups), out_shape=jax.ShapeDtyp...  30.1 us
    unnamed x1, local copies, waits for them, and re-layouts  1.57 us

profile of v4, /device:TPU:0, one launch (start us, length us, event | category | flops | bytes accessed | tf_op | source)
XLA Modules:
  0.0 31.7 jit_solution(5232190284865498910)
XLA Ops:
  0.0 30.1 %poisson_gradient.1 = f32[8,16,256]{2,1,0:T(8,128)} custom-call(bf16[8,16,256]{2,1,0:T(8,128)(2,1)} %act_hbm.1, s32[2,64,16,256]{3,2,1,0:T(8,128)} %counts_ref.1, bf16[2,16,256]{2,1,0:T(8,128)(2,1)} %back_hbm.1, bf16[6,32,256]{2,1,0:T(8,128)(2,1)} %bitcast.4, s32[3,2,256]{2,1,0:T(2,128)} %bitcast.5), custom_call_target="tpu_custom_call" | custom-call | tf_op jit(solution)/shard_map/poisson_gradient/pallas_call | solution.py:327
  30.1 1.6 %copy.7 = f32[8,16,256]{2,1,0:T(8,128)} copy(f32[8,16,256]{2,1,0:T(8,128)} %poisson_gradient.1) | data formatting | bytes 262144

commit v5 on v4

--- a/solution.py
+++ b/solution.py
@@ -286,14 +286,16 @@
             for copy in part_copies(step, met(last)):
                 copy.start()
 
-        @pl.when(step > 1)
-        def _():
-            pass_on(step - 1, kept_sum(step - 1) + pair_part(step - 1))
+        @pl.when(step > 2)
+        def _():
+            pass_on(step - 2, kept_sum(step - 2) + pair_part(step - 2))
 
         return carry
 
     lax.fori_loop(0, groups, one_group, 0)
     pass_on(last, kept_sum(last))
+    if last > 1:
+        pass_on(last - 1, kept_sum(last - 1) + pair_part(last - 1))
     gradient = kept_sum(0) + pair_part(0)
     for step in range(1, groups):
         for copy in sum_copies(step):

time: 31.8 us -> 32.6 us (1.025)
  Pallas kernels: 30.1 us -> 30.8 us
    pallas_call x1, Pallas kernels: 30.1 us -> 30.8 us  [per_device(): pl.pallas_call(functools.partial(kernel, groups), out_shape=jax.ShapeDtyp...]
where the time goes in v5:
time: 32.6 us; the launch traced here: 32.4 us
  Pallas kernels  30.8 us (94%)
  local copies, waits for them, and re-layouts  1.57 us (5%)
    pallas_call x1, Pallas kernels, per_device(): pl.pallas_call(functools.partial(kernel, groups), out_shape=jax.ShapeDtyp...  30.8 us
    unnamed x1, local copies, waits for them, and re-layouts  1.57 us

profile of v5, /device:TPU:0, one launch (start us, length us, event | category | flops | bytes accessed | tf_op | source)
XLA Modules:
  0.0 32.4 jit_solution(18108656072706212574)
XLA Ops:
  0.0 30.8 %poisson_gradient.1 = f32[8,16,256]{2,1,0:T(8,128)} custom-call(bf16[8,16,256]{2,1,0:T(8,128)(2,1)} %act_hbm.1, s32[2,64,16,256]{3,2,1,0:T(8,128)} %counts_ref.1, bf16[2,16,256]{2,1,0:T(8,128)(2,1)} %back_hbm.1, bf16[6,32,256]{2,1,0:T(8,128)(2,1)} %bitcast.4, s32[3,2,256]{2,1,0:T(2,128)} %bitcast.5), custom_call_target="tpu_custom_call" | custom-call | tf_op jit(solution)/shard_map/poisson_gradient/pallas_call | solution.py:329
  30.8 1.6 %copy.7 = f32[8,16,256]{2,1,0:T(8,128)} copy(f32[8,16,256]{2,1,0:T(8,128)} %poisson_gradient.1) | data formatting | bytes 262144

commit v6 on v4

--- a/solution.py
+++ b/solution.py
@@ -149,11 +149,11 @@
             device_id=at(met(step // PAIR), (lo + step % PAIR) % PAIR, 1 - slab), device_id_type=MESH,
         )
 
-    for step in range(members):
-        edge_copy(step).start()
     pair_copy(0, act_ref).start()
     for step in range(1, groups):
         line_copy(step).start()
+    for step in range(members):
+        edge_copy(step).start()
 
     slice_at = lax.broadcasted_iota(jnp.int32, (group_rows, slices, width), 1)
     inner = jnp.where(slab == 0, slices - 1, 0)

time: 31.8 us -> 31.3 us (0.984)
  Pallas kernels: 30.1 us -> 29.6 us
    pallas_call x1, Pallas kernels: 30.1 us -> 29.6 us  [per_device(): pl.pallas_call(functools.partial(kernel, groups), out_shape=jax.ShapeDtyp...]
where the time goes in v6:
time: 31.3 us; the launch traced here: 31.2 us
  Pallas kernels  29.6 us (95%)
  local copies, waits for them, and re-layouts  1.57 us (5%)
    pallas_call x1, Pallas kernels, per_device(): pl.pallas_call(functools.partial(kernel, groups), out_shape=jax.ShapeDtyp...  29.6 us
    unnamed x1, local copies, waits for them, and re-layouts  1.57 us

profile of v6, /device:TPU:0, one launch (start us, length us, event | category | flops | bytes accessed | tf_op | source)
XLA Modules:
  0.0 31.2 jit_solution(182040992243110451)
XLA Ops:
  0.0 29.6 %poisson_gradient.1 = f32[8,16,256]{2,1,0:T(8,128)} custom-call(bf16[8,16,256]{2,1,0:T(8,128)(2,1)} %act_hbm.1, s32[2,64,16,256]{3,2,1,0:T(8,128)} %counts_ref.1, bf16[2,16,256]{2,1,0:T(8,128)(2,1)} %back_hbm.1, bf16[6,32,256]{2,1,0:T(8,128)(2,1)} %bitcast.4, s32[3,2,256]{2,1,0:T(2,128)} %bitcast.5), custom_call_target="tpu_custom_call" | custom-call | tf_op jit(solution)/shard_map/poisson_gradient/pallas_call | solution.py:327
  29.6 1.6 %copy.7 = f32[8,16,256]{2,1,0:T(8,128)} copy(f32[8,16,256]{2,1,0:T(8,128)} %poisson_gradient.1) | data formatting | bytes 262144
